TPU v7x, 32 devices: a whole 2x2x4 slice. The times are simulated.
32 devices in a mesh: seq: 8 (over z, x), ep: 4 (over y, core).
Axes of the slice: x: 2, y: 2, z: 4, core: 2. Of those that a mesh axis runs over, the one named last changes fastest.
Arguments:
- tokens: bfloat16 [1024, 2048], P('seq'), may hold values from -12 to 12
- attn_gain: float32 [2048], replicated, may hold values from 0.1 to 1.9
- w_query: bfloat16 [2048, 512], P(None, 'ep'), may hold values from -1 to 1
- w_key: bfloat16 [2048, 512], P(None, 'ep'), may hold values from -8 to 8
- w_value: bfloat16 [2048, 512], P(None, 'ep'), may hold values from -0.125 to 0.125
- w_out: bfloat16 [512, 2048], P('ep'), may hold values from -0.25 to 0.25
- moe_gain: float32 [2048], replicated, may hold values from 0.1 to 1.9
- expert_ids: int32 [1024, 6], P('seq'), may hold values from 0 to 15, all different within a row; in each aligned block of 128 rows (0 to 127, 128 to 255, ...) at most 52 rows name the same one
- route_weight: float32 [1024, 6], P('seq'), may hold values from 0.2 to 1
- w_gate: bfloat16 [5632, 2048], P(('seq', 'ep')), may hold values from -0.125 to 0.125
- w_up: bfloat16 [5632, 2048], P(('seq', 'ep')), may hold values from -0.125 to 0.125
- w_down: bfloat16 [5632, 2048], P(('seq', 'ep')), may hold values from -0.3125 to 0.3125
Outputs:
- layer_out: bfloat16 [1024, 2048], P(('seq', 'ep'))
Inputs may be any that keep to these rules, and one draw needn't show every extreme that they name: `expert_ids`: each frame names 6 different experts; among the frames of one block of 128 no expert is named by more than 52 frames, a bound that some block reaches.
All inputs are finite; a program needn't handle non-finite values.
Results may differ from a plain program's by a relative error of at most 0.0065.
Values may be sent and summed in bfloat16 or wider, within the bound.
A program may use at most 64 MiB of HBM per device.

v0:
```python
import math
import jax
import jax.numpy as jnp
from jax import lax
from jax.sharding import PartitionSpec as P

EXP_ROW = 2
SPAN = 4
epsilon = 1e-05


def shifted(shard, axis, by):
    devices = lax.axis_size(axis)
    pairs = [(i, i + by) for i in range(devices) if 0 <= i + by < devices]
    return lax.ppermute(shard, axis, pairs)


def root_norm(values, gain):
    mean_square = jnp.mean(values * values, axis=-1, keepdims=True)
    return values * lax.rsqrt(mean_square + epsilon) * gain


def body(
    tokens,
    attn_gain,
    w_query,
    w_key,
    w_value,
    w_out,
    moe_gain,
    expert_ids,
    route_weight,
    w_gate,
    w_up,
    w_down,
):
    tok_rows, model_width = tokens.shape
    head_size = w_query.shape[1]
    seq_count = lax.axis_size("seq")
    ep_count = lax.axis_size("ep")
    seq_place = lax.axis_index("seq")
    ep_place = lax.axis_index("ep")
    row_share = tok_rows // ep_count
    tok_float = tokens.astype(jnp.float32)
    normed = root_norm(tok_float, attn_gain).astype(jnp.bfloat16)
    query_vectors = jnp.dot(normed, w_query, preferred_element_type=jnp.float32).astype(
        jnp.bfloat16
    )
    keys = jnp.dot(normed, w_key, preferred_element_type=jnp.float32).astype(jnp.bfloat16)
    values = jnp.dot(normed, w_value, preferred_element_type=jnp.float32).astype(jnp.bfloat16)
    stacked = jnp.stack([keys, values])
    key_parts = []
    value_parts = []
    for distance in range(SPAN, 0, -1):
        earlier = shifted(stacked, "seq", distance)
        key_parts.append(earlier[0])
        value_parts.append(earlier[1])
    window_key_rows = jnp.concatenate(key_parts + [keys], axis=0)
    window_value_rows = jnp.concatenate(value_parts + [values], axis=0)
    attention_logits = lax.dot_general(
        query_vectors, window_key_rows, (((1,), (1,)), ((), ())), preferred_element_type=jnp.float32
    ) / math.sqrt(head_size)
    query_pos = jnp.arange(tok_rows, dtype=jnp.int32)[:, None]
    key_rel = jnp.arange((SPAN + 1) * tok_rows, dtype=jnp.int32)[None, :] - SPAN * tok_rows
    window_len = SPAN * tok_rows
    allowed = (
        (key_rel <= query_pos)
        & (key_rel > query_pos - window_len)
        & (seq_place * tok_rows + key_rel >= 0)
    )
    attention_logits = jnp.where(allowed, attention_logits, -1e30)
    peak = jnp.max(attention_logits, axis=-1, keepdims=True)
    expo = jnp.exp(attention_logits - peak)
    attention_probabilities = (expo / jnp.sum(expo, axis=-1, keepdims=True)).astype(jnp.bfloat16)
    attention_output = jnp.dot(
        attention_probabilities, window_value_rows, preferred_element_type=jnp.float32
    ).astype(jnp.bfloat16)
    head_terms = jnp.dot(attention_output, w_out, preferred_element_type=jnp.float32)
    attn_total = lax.psum(head_terms, "ep")
    residual = tok_float + attn_total
    moe_in = root_norm(residual, moe_gain).astype(jnp.bfloat16)
    resid_rows = lax.dynamic_slice_in_dim(residual, ep_place * row_share, row_share, 0)
    top_count = expert_ids.shape[1]
    experts_all = seq_count * EXP_ROW
    slices = ep_count // EXP_ROW
    expert_half = ep_place // slices
    capacity = tok_rows * top_count // experts_all + tok_rows // 32
    expert_iota = jnp.arange(experts_all, dtype=jnp.int32)
    chosen = (expert_ids[:, :, None] == expert_iota).astype(jnp.float32)
    counts = jnp.sum(chosen, axis=1)
    earlier_mask = (jnp.arange(tok_rows)[:, None] > jnp.arange(tok_rows)[None, :]).astype(
        jnp.float32
    )
    before = jnp.dot(
        earlier_mask, counts, precision=lax.Precision.HIGHEST, preferred_element_type=jnp.float32
    )
    slot_index = jnp.sum(chosen * before[:, None, :], axis=-1)
    own_pairs = expert_ids % EXP_ROW == expert_half
    flat_slot = (expert_ids // EXP_ROW).astype(jnp.float32) * capacity + slot_index
    slot_iota = jnp.arange(seq_count * capacity, dtype=jnp.float32)
    slot_hits = (flat_slot[:, :, None] == slot_iota) & own_pairs[:, :, None]
    dispatch = jnp.any(slot_hits, axis=1).astype(jnp.bfloat16)
    panels = lax.dot_general(
        dispatch, moe_in, (((0,), (0,)), ((), ())), preferred_element_type=jnp.float32
    )
    panels = panels.astype(jnp.bfloat16).reshape(seq_count, capacity, model_width)
    rate = route_weight.astype(jnp.bfloat16).astype(jnp.float32)
    combine = jnp.sum(jnp.where(slot_hits, rate[:, :, None], 0.0), axis=1).astype(jnp.bfloat16)
    arrived = lax.all_to_all(panels, "seq", split_axis=0, concat_axis=0, tiled=True)
    flat_rows = arrived.reshape(-1, model_width)
    gate = lax.dot_general(
        flat_rows, w_gate, (((1,), (1,)), ((), ())), preferred_element_type=jnp.float32
    )
    upward = lax.dot_general(
        flat_rows, w_up, (((1,), (1,)), ((), ())), preferred_element_type=jnp.float32
    )
    hidden = (jax.nn.silu(gate) * upward).astype(jnp.bfloat16)
    result = jnp.dot(hidden, w_down, preferred_element_type=jnp.float32).astype(jnp.bfloat16)
    expert_out = result.reshape(arrived.shape[0], arrived.shape[1], model_width)
    returned = lax.all_to_all(expert_out, "seq", split_axis=0, concat_axis=0, tiled=True)
    moe_terms = jnp.dot(
        combine, returned.reshape(-1, model_width), preferred_element_type=jnp.float32
    )
    moe_rows = lax.psum_scatter(moe_terms, "ep", scatter_dimension=0, tiled=True)
    return (resid_rows + moe_rows).astype(jnp.bfloat16)


def solution(mesh):
    in_specs = (
        P("seq", None),
        P(),
        P(None, "ep"),
        P(None, "ep"),
        P(None, "ep"),
        P("ep", None),
        P(),
        P("seq", None),
        P("seq", None),
        P(("seq", "ep"), None),
        P(("seq", "ep"), None),
        P(("seq", "ep"), None),
    )
    out_specs = P(("seq", "ep"), None)
    return jax.shard_map(body, mesh=mesh, in_specs=in_specs, out_specs=out_specs, check_vma=False)
```

profile of v0, /device:TPU:0, one launch (start us, length us, event | category | flops | bytes accessed | tf_op | source)
XLA Modules:
  0.0 210.8 jit_solution(13454979332110237027)
XLA Ops:
  6.6 1.3 fusion.5
  8.0 1.6 convolution_convert_fusion.4
  10.0 6.1 %collective-permute-start = (bf16[2,128,128]{2,1,0:T(8,128)(2,1)S(1)}, bf16[2,128,128]{2,1,0:T(8,128)(2,1)S(1)}, u32[]{:S(2)}, u32[]{:S(2)}) collective-permute-start(bf16[2,128,128]{2,1,0:T(8,128)(2,1)S(1)} %pad_maximum_fusion), channel_id=1, source_target_pairs={{0,16},{4,20},{8,24},{12,28},{1,17},{5,21},{9,25},{13,29},{2,18},{... | collective-permute-start | bytes 196616 | tf_op jit(solution)/shard_map/ppermute | solution.py:15
  16.1 4.4 %collective-permute-start.1 = (bf16[2,128,128]{2,1,0:T(8,128)(2,1)S(1)}, bf16[2,128,128]{2,1,0:T(8,128)(2,1)S(1)}, u32[]{:S(2)}, u32[]{:S(2)}) collective-permute-start(bf16[2,128,128]{2,1,0:T(8,128)(2,1)S(1)} %pad_maximum_fusion), channel_id=1, source_target_pairs={{0,12},{4,16},{8,20},{12,24},{16,28},{1,13},{5,17},{9,21},{13,25},... | collective-permute-start | bytes 196616 | tf_op jit(solution)/shard_map/ppermute | solution.py:15
  20.6 1.3 collective-permute-start.2
  21.9 3.1 %collective-permute-start.3 = (bf16[2,128,128]{2,1,0:T(8,128)(2,1)S(1)}, bf16[2,128,128]{2,1,0:T(8,128)(2,1)S(1)}, u32[]{:S(2)}, u32[]{:S(2)}) collective-permute-start(bf16[2,128,128]{2,1,0:T(8,128)(2,1)S(1)} %pad_maximum_fusion), channel_id=1, source_target_pairs={{0,4},{4,8},{8,12},{12,16},{16,20},{20,24},{24,28},{1,5},{5,9},{9,... | collective-permute-start | bytes 196616 | tf_op jit(solution)/shard_map/ppermute | solution.py:15
  25.3 1.5 collective-permute-done.3
  27.7 1.6 fusion.4
  29.6 35.5 %all-reduce.2.cloned.1.call-done = f32[128,2048]{1,0:T(8,128)} async-done(((f32[128,2048]{1,0:T(8,128)}), f32[128,2048]{1,0:T(8,128)}) %all-reduce.2.cloned.1.call-update) | async-done | bytes 1048592 | tf_op jit(solution)/shard_map/psum | solution.py:79
  65.1 1.4 multiply_reduce_fusion
  66.6 1.0 copy-done.1
  67.6 1.9 convolution_convert_fusion.1
  69.4 1.6 reshape.52
  71.0 47.5 %all_to_all.10 = bf16[8,52,2048]{2,1,0:T(8,128)(2,1)} all-to-all(bf16[8,52,2048]{2,1,0:T(8,128)(2,1)S(1)} %reshape.52), channel_id=1, replica_groups=mesh['seq'=8,'ep'=4] {'seq'}, dimensions={0} | all-to-all | bytes 3407872 | tf_op jit(solution)/shard_map/all_to_all | solution.py:109
  118.6 1.7 reshape.53
  120.3 1.4 fusion.48
  121.7 3.9 %convolution_convert_fusion = bf16[416,2048]{1,0:T(8,128)(2,1)} fusion(bf16[176,2048]{1,0:T(8,128)(2,1)S(1)} %copy-done, bf16[416,2048]{1,0:T(8,128)(2,1)S(1)} %reshape.53, bf16[176,2048]{1,0:T(8,128)(2,1)} %param.22, f32[416,176]{0,1:T(8,128)} %fusion.48), kind=kOutput, calls=%fused_computation | convolution fusion | flops 601076736 | bytes 5142528 | tf_op jit(solution)/shard_map/dot_general | solution.py:118
  125.6 2.6 %reshape.54 = bf16[8,52,2048]{2,1,0:T(8,128)(2,1)} reshape(bf16[416,2048]{1,0:T(8,128)(2,1)} %convolution_convert_fusion) | data formatting | bytes 3407872 | tf_op jit(solution)/shard_map/reshape | solution.py:119
  128.1 3.7 %all-to-all-start.1 = ((bf16[8,52,2048]{2,1,0:T(8,128)(2,1)}), bf16[8,52,2048]{2,1,0:T(8,128)(2,1)S(1)}, u32[]{:S(2)}, u32[]{:S(2)}) async-start(bf16[8,52,2048]{2,1,0:T(8,128)(2,1)} %reshape.54), calls=%async_computation.1 | async-start | bytes 3670016 | tf_op jit(solution)/shard_map/all_to_all | solution.py:120
  132.2 41.7 %all-to-all-done.1 = bf16[8,52,2048]{2,1,0:T(8,128)(2,1)S(1)} async-done(((bf16[8,52,2048]{2,1,0:T(8,128)(2,1)}), bf16[8,52,2048]{2,1,0:T(8,128)(2,1)S(1)}, u32[]{:S(2)}, u32[]{:S(2)}) %all-to-all-start.1) | async-done | bytes 1703968 | tf_op jit(solution)/shard_map/all_to_all | solution.py:120
  174.0 1.4 reshape.55
  175.3 2.9 %fusion.49 = f32[128,2048]{1,0:T(8,128)} fusion(bf16[128,416]{0,1:T(8,128)(2,1)S(1)} %select_reduce_fusion, bf16[416,2048]{1,0:T(8,128)(2,1)} %reshape.55), kind=kOutput, calls=%fused_computation.87 | convolution fusion | flops 218103808 | bytes 2859008 | tf_op jit(solution)/shard_map/dot_general | solution.py:121
  178.3 24.0 %reduce-scatter.2.cloned.1.call-done = f32[32,2048]{1,0:T(8,128)} async-done(((f32[128,2048]{1,0:T(8,128)}), f32[32,2048]{1,0:T(8,128)}) %reduce-scatter.2.cloned.1.call-update) | async-done | bytes 262160 | tf_op jit(solution)/shard_map/reduce_scatter | solution.py:124
  202.3 1.7 add_convert_fusion
  (50 shorter events, 2.2 us)
Async XLA Ops:
  6.5 115.2 %copy-start = (bf16[176,2048]{1,0:T(8,128)(2,1)S(1)}, bf16[176,2048]{1,0:T(8,128)(2,1)}, u32[]{:S(2)}) copy-start(bf16[176,2048]{1,0:T(8,128)(2,1)} %param.23) | copy-start | bytes 2162692
  6.5 3.1 %copy-start.2 = (bf16[128,2048]{1,0:T(8,128)(2,1)S(1)}, bf16[128,2048]{1,0:T(8,128)(2,1)}, u32[]{:S(2)}) copy-start(bf16[128,2048]{1,0:T(8,128)(2,1)} %param.12) | copy-start | bytes 1572868
  6.5 3.1 %copy-start.10 = (f32[2048]{0:T(1024)S(1)}, f32[2048]{0:T(1024)}, u32[]{:S(2)}) copy-start(f32[2048]{0:T(1024)} %param.13) | copy-start | bytes 24580
  6.5 3.1 %copy-start.8 = (bf16[2048,128]{1,0:T(8,128)(2,1)S(1)}, bf16[2048,128]{1,0:T(8,128)(2,1)}, u32[]{:S(2)}) copy-start(bf16[2048,128]{1,0:T(8,128)(2,1)} %param.16) | copy-start | bytes 1572868
  6.5 18.5 %copy-start.4 = (s32[128,6]{0,1:T(8,128)S(1)}, s32[128,6]{0,1:T(8,128)}, u32[]{:S(2)}) copy-start(s32[128,6]{0,1:T(8,128)} %param.19) | copy-start | bytes 9220
  6.5 58.6 %all-reduce.2.cloned.1.call-start = ((), (), s32[]{:S(2)}) async-start(), calls=%async_computation.3 | async-start | bytes 2097152 | tf_op jit(solution)/shard_map/psum | solution.py:79
  8.0 18.9 %copy-start.9 = (bf16[2048,128]{1,0:T(8,128)(2,1)S(1)}, bf16[2048,128]{1,0:T(8,128)(2,1)}, u32[]{:S(2)}) copy-start(bf16[2048,128]{1,0:T(8,128)(2,1)} %param.14) | copy-start | bytes 1572868
  10.0 17.7 %copy-start.3 = (bf16[128,2048]{1,0:T(8,128)(2,1)S(1)}, bf16[128,2048]{1,0:T(8,128)(2,1)}, u32[]{:S(2)}) copy-start(bf16[128,2048]{1,0:T(8,128)(2,1)} %param.17) | copy-start | bytes 1572868
  10.0 15.2 %collective-permute-start = (bf16[2,128,128]{2,1,0:T(8,128)(2,1)S(1)}, bf16[2,128,128]{2,1,0:T(8,128)(2,1)S(1)}, u32[]{:S(2)}, u32[]{:S(2)}) collective-permute-start(bf16[2,128,128]{2,1,0:T(8,128)(2,1)S(1)} %pad_maximum_fusion), channel_id=1, source_target_pairs={{0,16},{4,20},{8,24},{12,28},{1,17},{5,21},{9,25},{13,29},{2,18},{... | collective-permute-start | bytes 196616 | tf_op jit(solution)/shard_map/ppermute | solution.py:15
  16.1 9.1 %collective-permute-start.1 = (bf16[2,128,128]{2,1,0:T(8,128)(2,1)S(1)}, bf16[2,128,128]{2,1,0:T(8,128)(2,1)S(1)}, u32[]{:S(2)}, u32[]{:S(2)}) collective-permute-start(bf16[2,128,128]{2,1,0:T(8,128)(2,1)S(1)} %pad_maximum_fusion), channel_id=1, source_target_pairs={{0,12},{4,16},{8,20},{12,24},{16,28},{1,13},{5,17},{9,21},{13,25},... | collective-permute-start | bytes 196616 | tf_op jit(solution)/shard_map/ppermute | solution.py:15
  20.6 4.7 %collective-permute-start.2 = (bf16[2,128,128]{2,1,0:T(8,128)(2,1)S(1)}, bf16[2,128,128]{2,1,0:T(8,128)(2,1)S(1)}, u32[]{:S(2)}, u32[]{:S(2)}) collective-permute-start(bf16[2,128,128]{2,1,0:T(8,128)(2,1)S(1)} %pad_maximum_fusion), channel_id=1, source_target_pairs={{0,8},{4,12},{8,16},{12,20},{16,24},{20,28},{1,9},{5,13},{9,17},{1... | collective-permute-start | bytes 196616 | tf_op jit(solution)/shard_map/ppermute | solution.py:15
  21.9 5.0 %collective-permute-start.3 = (bf16[2,128,128]{2,1,0:T(8,128)(2,1)S(1)}, bf16[2,128,128]{2,1,0:T(8,128)(2,1)S(1)}, u32[]{:S(2)}, u32[]{:S(2)}) collective-permute-start(bf16[2,128,128]{2,1,0:T(8,128)(2,1)S(1)} %pad_maximum_fusion), channel_id=1, source_target_pairs={{0,4},{4,8},{8,12},{12,16},{16,20},{20,24},{24,28},{1,5},{5,9},{9,... | collective-permute-start | bytes 196616 | tf_op jit(solution)/shard_map/ppermute | solution.py:15
  29.3 38.3 %copy-start.5 = (f32[2048]{0:T(1024)S(1)}, f32[2048]{0:T(1024)}, u32[]{:S(2)}) copy-start(f32[2048]{0:T(1024)} %param.18) | copy-start | bytes 24580
  66.6 1.0 copy-start.1
  118.6 1.7 copy-start.7
  128.1 3.8 %copy-start.6 = (f32[128,6]{0,1:T(8,128)S(1)}, f32[128,6]{0,1:T(8,128)}, u32[]{:S(2)}) copy-start(f32[128,6]{0,1:T(8,128)} %param.20) | copy-start | bytes 9220
  128.1 45.8 %all-to-all-start.1 = ((bf16[8,52,2048]{2,1,0:T(8,128)(2,1)}), bf16[8,52,2048]{2,1,0:T(8,128)(2,1)S(1)}, u32[]{:S(2)}, u32[]{:S(2)}) async-start(bf16[8,52,2048]{2,1,0:T(8,128)(2,1)} %reshape.54), calls=%async_computation.1 | async-start | bytes 3670016 | tf_op jit(solution)/shard_map/all_to_all | solution.py:120
  131.9 70.4 %reduce-scatter.2.cloned.1.call-start = ((), (), s32[]{:S(2)}) async-start(), calls=%async_computation.4 | async-start | bytes 1310720 | tf_op jit(solution)/shard_map/reduce_scatter | solution.py:124
Sparse Core Ops, SparseCore 0:
  29.4 35.6 all-reduce.1
  178.4 23.8 reduce-scatter.1
where the time goes:
time: 211 us
  waiting for transfers between devices  103 us (49%)
  blocking collectives  47.5 us (23%)
  starting transfers between devices  18.7 us (9%)
  matrix products  14.3 us (7%)
  between operations  13.7 us (6%)
  local copies, waits for them, and re-layouts  8.3 us (4%)
  other arithmetic  5.34 us (3%)
    all_to_all x1, blocking collectives, body(): lax.all_to_all(panels, 'seq', split_axis=0, concat_axis=0, tiled=True)  47.5 us
    all_to_all x1, waiting for transfers between devices, body(): lax.all_to_all(expert_out, 'seq', split_axis=0, concat_axis=0, tiled=True)  41.7 us
    psum x1, waiting for transfers between devices, body(): attn_total = lax.psum(head_terms, 'ep')  35.5 us
    reduce_scatter x1, waiting for transfers between devices, body(): lax.psum_scatter(moe_terms, 'ep', scatter_dimension=0, tiled=True)  24 us
    ppermute x4, starting transfers between devices, shifted(): return lax.ppermute(shard, axis, pairs)  14.9 us
  transfers between devices with their start and end apart: 7, of which 4 were waited for; matrix products, arithmetic and copies ran while one was open for 0% of the time, Pallas kernels for 0%

commit v1 on v0

--- a/solution.py
+++ b/solution.py
@@ -76,7 +76,7 @@
         attention_probabilities, window_value_rows, preferred_element_type=jnp.float32
     ).astype(jnp.bfloat16)
     head_terms = jnp.dot(attention_output, w_out, preferred_element_type=jnp.float32)
-    attn_total = lax.psum(head_terms, "ep")
+    attn_total = jnp.sum(lax.all_gather(head_terms, "ep"), axis=0)
     residual = tok_float + attn_total
     moe_in = root_norm(residual, moe_gain).astype(jnp.bfloat16)
     resid_rows = lax.dynamic_slice_in_dim(residual, ep_place * row_share, row_share, 0)

time: 211 us -> 211 us (level)
    psum x1 -> x0, waiting for transfers between devices: 35.5 us -> none  [body(): attn_total = lax.psum(head_terms, 'ep')]
    all_gather x0 -> x1, waiting for transfers between devices: none -> 33.5 us  [body(): attn_total = jnp.sum(lax.all_gather(head_terms, 'ep'), axis=0)]
    reduce_sum x0 -> x1, other arithmetic: none -> 2.6 us  [body(): attn_total = jnp.sum(lax.all_gather(head_terms, 'ep'), axis=0)]
where the time goes in v1:
time: 211 us
  waiting for transfers between devices  101 us (48%)
  blocking collectives  48.4 us (23%)
  starting transfers between devices  18.7 us (9%)
  matrix products  14.3 us (7%)
  between operations  13.7 us (6%)
  local copies, waits for them, and re-layouts  8.31 us (4%)
  other arithmetic  6.77 us (3%)
    all_to_all x1, blocking collectives, body(): lax.all_to_all(panels, 'seq', split_axis=0, concat_axis=0, tiled=True)  48.4 us
    all_to_all x1, waiting for transfers between devices, body(): lax.all_to_all(expert_out, 'seq', split_axis=0, concat_axis=0, tiled=True)  42.2 us
    all_gather x1, waiting for transfers between devices, body(): attn_total = jnp.sum(lax.all_gather(head_terms, 'ep'), axis=0)  33.5 us
    reduce_scatter x1, waiting for transfers between devices, body(): lax.psum_scatter(moe_terms, 'ep', scatter_dimension=0, tiled=True)  23.1 us
    ppermute x4, starting transfers between devices, shifted(): return lax.ppermute(shard, axis, pairs)  14.9 us
  transfers between devices with their start and end apart: 7, of which 4 were waited for; matrix products, arithmetic and copies ran while one was open for 0% of the time, Pallas kernels for 0%

profile of v1, /device:TPU:0, one launch (start us, length us, event | category | flops | bytes accessed | tf_op | source)
XLA Modules:
  0.0 210.8 jit_solution(2641358039041187021)
XLA Ops:
  6.6 1.4 fusion.5
  8.0 1.6 convolution_convert_fusion.4
  10.0 6.1 %collective-permute-start = (bf16[2,128,128]{2,1,0:T(8,128)(2,1)S(1)}, bf16[2,128,128]{2,1,0:T(8,128)(2,1)S(1)}, u32[]{:S(2)}, u32[]{:S(2)}) collective-permute-start(bf16[2,128,128]{2,1,0:T(8,128)(2,1)S(1)} %pad_maximum_fusion), channel_id=1, source_target_pairs={{0,16},{4,20},{8,24},{12,28},{1,17},{5,21},{9,25},{13,29},{2,18},{... | collective-permute-start | bytes 196616 | tf_op jit(solution)/shard_map/ppermute | solution.py:15
  16.1 4.4 %collective-permute-start.1 = (bf16[2,128,128]{2,1,0:T(8,128)(2,1)S(1)}, bf16[2,128,128]{2,1,0:T(8,128)(2,1)S(1)}, u32[]{:S(2)}, u32[]{:S(2)}) collective-permute-start(bf16[2,128,128]{2,1,0:T(8,128)(2,1)S(1)} %pad_maximum_fusion), channel_id=1, source_target_pairs={{0,12},{4,16},{8,20},{12,24},{16,28},{1,13},{5,17},{9,21},{13,25},... | collective-permute-start | bytes 196616 | tf_op jit(solution)/shard_map/ppermute | solution.py:15
  20.5 1.3 collective-permute-start.2
  21.8 3.1 %collective-permute-start.3 = (bf16[2,128,128]{2,1,0:T(8,128)(2,1)S(1)}, bf16[2,128,128]{2,1,0:T(8,128)(2,1)S(1)}, u32[]{:S(2)}, u32[]{:S(2)}) collective-permute-start(bf16[2,128,128]{2,1,0:T(8,128)(2,1)S(1)} %pad_maximum_fusion), channel_id=1, source_target_pairs={{0,4},{4,8},{8,12},{12,16},{16,20},{20,24},{24,28},{1,5},{5,9},{9,... | collective-permute-start | bytes 196616 | tf_op jit(solution)/shard_map/ppermute | solution.py:15
  25.1 1.8 collective-permute-done.3
  27.7 1.5 fusion.4
  29.8 33.5 %all-gather.3.cloned.1.call-done = f32[512,2048]{1,0:T(8,128)} async-done(((f32[128,2048]{1,0:T(8,128)}), f32[512,2048]{1,0:T(8,128)}) %all-gather.3.cloned.1.call-update) | async-done | bytes 4194320 | tf_op jit(solution)/shard_map/all_gather | solution.py:79
  63.2 2.6 %reduce_sum.65 = f32[128,2048]{1,0:T(8,128)S(1)} reduce(f32[4,128,2048]{2,1,0:T(8,128)} %bitcast.50, f32[]{:T(128)} %constant.64.clone.1), dimensions={0}, to_apply=%region_3.4 | reduce | flops 786432 | bytes 5242884 | tf_op jit(solution)/shard_map/reduce_sum | solution.py:79
  66.1 1.0 copy-done.1
  67.0 1.9 convolution_convert_fusion.1
  68.9 1.6 reshape.52
  70.5 48.4 %all_to_all.10 = bf16[8,52,2048]{2,1,0:T(8,128)(2,1)} all-to-all(bf16[8,52,2048]{2,1,0:T(8,128)(2,1)S(1)} %reshape.52), channel_id=1, replica_groups=mesh['seq'=8,'ep'=4] {'seq'}, dimensions={0} | all-to-all | bytes 3407872 | tf_op jit(solution)/shard_map/all_to_all | solution.py:109
  118.9 1.7 reshape.53
  120.6 1.4 fusion.48
  122.0 3.9 %convolution_convert_fusion = bf16[416,2048]{1,0:T(8,128)(2,1)} fusion(bf16[176,2048]{1,0:T(8,128)(2,1)S(1)} %copy-done, bf16[416,2048]{1,0:T(8,128)(2,1)S(1)} %reshape.53, bf16[176,2048]{1,0:T(8,128)(2,1)} %param.22, f32[416,176]{0,1:T(8,128)} %fusion.48), kind=kOutput, calls=%fused_computation | convolution fusion | flops 601076736 | bytes 5142528 | tf_op jit(solution)/shard_map/dot_general | solution.py:118
  125.9 2.6 %reshape.54 = bf16[8,52,2048]{2,1,0:T(8,128)(2,1)} reshape(bf16[416,2048]{1,0:T(8,128)(2,1)} %convolution_convert_fusion) | data formatting | bytes 3407872 | tf_op jit(solution)/shard_map/reshape | solution.py:119
  128.5 3.8 %all-to-all-start.1 = ((bf16[8,52,2048]{2,1,0:T(8,128)(2,1)}), bf16[8,52,2048]{2,1,0:T(8,128)(2,1)S(1)}, u32[]{:S(2)}, u32[]{:S(2)}) async-start(bf16[8,52,2048]{2,1,0:T(8,128)(2,1)} %reshape.54), calls=%async_computation.1 | async-start | bytes 3670016 | tf_op jit(solution)/shard_map/all_to_all | solution.py:120
  132.6 42.2 %all-to-all-done.1 = bf16[8,52,2048]{2,1,0:T(8,128)(2,1)S(1)} async-done(((bf16[8,52,2048]{2,1,0:T(8,128)(2,1)}), bf16[8,52,2048]{2,1,0:T(8,128)(2,1)S(1)}, u32[]{:S(2)}, u32[]{:S(2)}) %all-to-all-start.1) | async-done | bytes 1703968 | tf_op jit(solution)/shard_map/all_to_all | solution.py:120
  174.8 1.4 reshape.55
  176.2 2.9 %fusion.49 = f32[128,2048]{1,0:T(8,128)} fusion(bf16[128,416]{0,1:T(8,128)(2,1)S(1)} %select_reduce_fusion, bf16[416,2048]{1,0:T(8,128)(2,1)} %reshape.55), kind=kOutput, calls=%fused_computation.87 | convolution fusion | flops 218103808 | bytes 2859008 | tf_op jit(solution)/shard_map/dot_general | solution.py:121
  179.1 23.1 %reduce-scatter.2.cloned.1.call-done = f32[32,2048]{1,0:T(8,128)} async-done(((f32[128,2048]{1,0:T(8,128)}), f32[32,2048]{1,0:T(8,128)}) %reduce-scatter.2.cloned.1.call-update) | async-done | bytes 262160 | tf_op jit(solution)/shard_map/reduce_scatter | solution.py:124
  202.2 1.7 add_convert_fusion
  (51 shorter events, 2.4 us)
Async XLA Ops:
  6.5 115.5 %copy-start = (bf16[176,2048]{1,0:T(8,128)(2,1)S(1)}, bf16[176,2048]{1,0:T(8,128)(2,1)}, u32[]{:S(2)}) copy-start(bf16[176,2048]{1,0:T(8,128)(2,1)} %param.23) | copy-start | bytes 2162692
  6.5 3.1 %copy-start.2 = (bf16[128,2048]{1,0:T(8,128)(2,1)S(1)}, bf16[128,2048]{1,0:T(8,128)(2,1)}, u32[]{:S(2)}) copy-start(bf16[128,2048]{1,0:T(8,128)(2,1)} %param.12) | copy-start | bytes 1572868
  6.5 3.1 %copy-start.10 = (f32[2048]{0:T(1024)S(1)}, f32[2048]{0:T(1024)}, u32[]{:S(2)}) copy-start(f32[2048]{0:T(1024)} %param.13) | copy-start | bytes 24580
  6.5 3.1 %copy-start.8 = (bf16[2048,128]{1,0:T(8,128)(2,1)S(1)}, bf16[2048,128]{1,0:T(8,128)(2,1)}, u32[]{:S(2)}) copy-start(bf16[2048,128]{1,0:T(8,128)(2,1)} %param.16) | copy-start | bytes 1572868
  6.5 56.7 %all-gather.3.cloned.1.call-start = ((), (), s32[]{:S(2)}) async-start(), calls=%async_computation.4 | async-start | bytes 5242880 | tf_op jit(solution)/shard_map/all_gather | solution.py:79
  7.9 18.9 %copy-start.9 = (bf16[2048,128]{1,0:T(8,128)(2,1)S(1)}, bf16[2048,128]{1,0:T(8,128)(2,1)}, u32[]{:S(2)}) copy-start(bf16[2048,128]{1,0:T(8,128)(2,1)} %param.14) | copy-start | bytes 1572868
  10.0 17.7 %copy-start.3 = (bf16[128,2048]{1,0:T(8,128)(2,1)S(1)}, bf16[128,2048]{1,0:T(8,128)(2,1)}, u32[]{:S(2)}) copy-start(bf16[128,2048]{1,0:T(8,128)(2,1)} %param.17) | copy-start | bytes 1572868
  10.0 15.0 %collective-permute-start = (bf16[2,128,128]{2,1,0:T(8,128)(2,1)S(1)}, bf16[2,128,128]{2,1,0:T(8,128)(2,1)S(1)}, u32[]{:S(2)}, u32[]{:S(2)}) collective-permute-start(bf16[2,128,128]{2,1,0:T(8,128)(2,1)S(1)} %pad_maximum_fusion), channel_id=1, source_target_pairs={{0,16},{4,20},{8,24},{12,28},{1,17},{5,21},{9,25},{13,29},{2,18},{... | collective-permute-start | bytes 196616 | tf_op jit(solution)/shard_map/ppermute | solution.py:15
  16.1 8.9 %collective-permute-start.1 = (bf16[2,128,128]{2,1,0:T(8,128)(2,1)S(1)}, bf16[2,128,128]{2,1,0:T(8,128)(2,1)S(1)}, u32[]{:S(2)}, u32[]{:S(2)}) collective-permute-start(bf16[2,128,128]{2,1,0:T(8,128)(2,1)S(1)} %pad_maximum_fusion), channel_id=1, source_target_pairs={{0,12},{4,16},{8,20},{12,24},{16,28},{1,13},{5,17},{9,21},{13,25},... | collective-permute-start | bytes 196616 | tf_op jit(solution)/shard_map/ppermute | solution.py:15
  20.5 4.5 %collective-permute-start.2 = (bf16[2,128,128]{2,1,0:T(8,128)(2,1)S(1)}, bf16[2,128,128]{2,1,0:T(8,128)(2,1)S(1)}, u32[]{:S(2)}, u32[]{:S(2)}) collective-permute-start(bf16[2,128,128]{2,1,0:T(8,128)(2,1)S(1)} %pad_maximum_fusion), channel_id=1, source_target_pairs={{0,8},{4,12},{8,16},{12,20},{16,24},{20,28},{1,9},{5,13},{9,17},{1... | collective-permute-start | bytes 196616 | tf_op jit(solution)/shard_map/ppermute | solution.py:15
  21.8 5.0 %collective-permute-start.3 = (bf16[2,128,128]{2,1,0:T(8,128)(2,1)S(1)}, bf16[2,128,128]{2,1,0:T(8,128)(2,1)S(1)}, u32[]{:S(2)}, u32[]{:S(2)}) collective-permute-start(bf16[2,128,128]{2,1,0:T(8,128)(2,1)S(1)} %pad_maximum_fusion), channel_id=1, source_target_pairs={{0,4},{4,8},{8,12},{12,16},{16,20},{20,24},{24,28},{1,5},{5,9},{9,... | collective-permute-start | bytes 196616 | tf_op jit(solution)/shard_map/ppermute | solution.py:15
  27.5 1.8 copy-start.4
  65.8 1.2 copy-start.5
  66.1 1.0 copy-start.1
  118.9 1.7 copy-start.7
  128.5 3.8 %copy-start.6 = (f32[128,6]{0,1:T(8,128)S(1)}, f32[128,6]{0,1:T(8,128)}, u32[]{:S(2)}) copy-start(f32[128,6]{0,1:T(8,128)} %param.20) | copy-start | bytes 9220
  128.5 46.4 %all-to-all-start.1 = ((bf16[8,52,2048]{2,1,0:T(8,128)(2,1)}), bf16[8,52,2048]{2,1,0:T(8,128)(2,1)S(1)}, u32[]{:S(2)}, u32[]{:S(2)}) async-start(bf16[8,52,2048]{2,1,0:T(8,128)(2,1)} %reshape.54), calls=%async_computation.1 | async-start | bytes 3670016 | tf_op jit(solution)/shard_map/all_to_all | solution.py:120
  132.2 70.0 %reduce-scatter.2.cloned.1.call-start = ((), (), s32[]{:S(2)}) async-start(), calls=%async_computation.3 | async-start | bytes 1310720 | tf_op jit(solution)/shard_map/reduce_scatter | solution.py:124
Sparse Core Ops, SparseCore 0:
  29.4 33.8 all-gather.2
  179.2 22.9 reduce-scatter.1
